TPU v7x, 32 devices: a whole 2x2x4 slice. The times are simulated.
32 devices in a mesh: bag: 4 (over x, core), sp: 8 (over z, y).
Axes of the slice: x: 2, y: 2, z: 4, core: 2. Of those that a mesh axis runs over, the one named last changes fastest.
Arguments:
- tokens: bfloat16 [8192, 1152], P(('bag', 'sp')), may hold values from -8 to 8
- row_seq: int32 [8192], P(('bag', 'sp')), may hold values from 0 to 3, as said below
- modulation: float32 [4, 6, 1152], replicated, may hold values from -4 to 4
- w_qkv: bfloat16 [1152, 3456], replicated, may hold values from -1 to 1
- w_out: bfloat16 [1152, 1152], replicated, may hold values from -0.1875 to 0.1875
- w_fc1: bfloat16 [1152, 2304], replicated, may hold values from -0.1875 to 0.1875
- w_fc2: bfloat16 [2304, 1152], replicated, may hold values from -0.125 to 0.125
Outputs:
- output: bfloat16 [8192, 1152], P(('bag', 'sp'))
Inputs may be any that keep to these rules, and one draw needn't show every extreme that they name: `row_seq`: rows 2m and 2m + 1 belong to the same sequence. Sequence s lies in bag s. Of one device's 256 rows at most 80 lie in any one bag, and on every device exactly 80 lie in one bag. Every sequence has rows.
All inputs are finite; a program needn't handle non-finite values.
Results may differ from a plain program's by a relative error of at most 0.0095.
Values may be sent and summed in bfloat16 or wider, within the bound.
No kernel may reach another device: no remote copies, remote signals or barrier semaphores. Data moves between devices by JAX's collectives and lax.ppermute only.
A program may use at most 128 MiB of HBM per device.

v0:
```python
import math
import jax
import jax.numpy as jnp
from jax import lax
from jax.sharding import PartitionSpec as P

HD = 72
SEQ_BAG = 1
EPS = 1e-06


def layer_norm(values):
    center = values - jnp.mean(values, axis=-1, keepdims=True)
    spread = jnp.mean(center * center, axis=-1, keepdims=True)
    return center * lax.rsqrt(spread + EPS)


def lookup(seq_codes, modulation):
    seq_total = modulation.shape[0]
    one_hot = (seq_codes[:, None] == jnp.arange(seq_total, dtype=jnp.int32)[None, :]).astype(
        jnp.float32
    )
    table_rows = modulation.reshape(seq_total, -1)
    picked = jnp.dot(
        one_hot, table_rows, precision=lax.Precision.HIGHEST, preferred_element_type=jnp.float32
    )
    return picked.reshape(seq_codes.shape[0], 6, -1)


def project(source_rows, mods, w_qkv):
    normed = (layer_norm(source_rows.astype(jnp.float32)) * (1.0 + mods[:, 1]) + mods[:, 0]).astype(
        jnp.bfloat16
    )
    return jnp.dot(normed, w_qkv, preferred_element_type=jnp.float32).astype(jnp.bfloat16)


def attend(packed, seq_codes):
    key_count = packed.shape[0]
    local_width = packed.shape[2]
    head_local = local_width // HD
    queries = packed[:, 0].reshape(key_count, head_local, HD)
    key_rows = packed[:, 1].reshape(key_count, head_local, HD)
    values = packed[:, 2].reshape(key_count, head_local, HD)
    block_size = math.gcd(key_count, 512)
    score_scale = 1.0 / math.sqrt(HD)

    def one_block(block_index):
        first_row = block_index * block_size
        query_part = lax.dynamic_slice_in_dim(queries, first_row, block_size, 0)
        query_seq = lax.dynamic_slice_in_dim(seq_codes, first_row, block_size, 0)
        scores = (
            jnp.einsum("qhd,khd->hqk", query_part, key_rows, preferred_element_type=jnp.float32)
            * score_scale
        )
        allowed = query_seq[:, None] == seq_codes[None, :]
        scores = jnp.where(allowed[None], scores, -jnp.inf)
        row_max = jnp.max(scores, axis=-1, keepdims=True)
        raised = jnp.exp(scores - row_max)
        denominator = jnp.sum(raised, axis=-1)
        probs = raised.astype(jnp.bfloat16)
        mixed_rows = jnp.einsum("hqk,khd->qhd", probs, values, preferred_element_type=jnp.float32)
        mixed_rows = mixed_rows / jnp.transpose(denominator)[:, :, None]
        return mixed_rows.astype(jnp.bfloat16).reshape(block_size, local_width)

    blocks = lax.map(one_block, jnp.arange(key_count // block_size, dtype=jnp.int32))
    return blocks.reshape(key_count, local_width)


def finish(residual, attended, mods, w_out, w_fc1, w_fc2):
    branch = jnp.dot(attended, w_out, preferred_element_type=jnp.float32)
    hidden = (residual.astype(jnp.float32) + mods[:, 2] * branch).astype(jnp.bfloat16)
    normed = (layer_norm(hidden.astype(jnp.float32)) * (1.0 + mods[:, 4]) + mods[:, 3]).astype(
        jnp.bfloat16
    )
    active = jax.nn.gelu(
        jnp.dot(normed, w_fc1, preferred_element_type=jnp.float32), approximate=True
    ).astype(jnp.bfloat16)
    return (
        hidden.astype(jnp.float32)
        + mods[:, 5] * jnp.dot(active, w_fc2, preferred_element_type=jnp.float32)
    ).astype(jnp.bfloat16)


def shards(tokens, row_seq, modulation, w_qkv, w_out, w_fc1, w_fc2):
    bag_count = lax.axis_size("bag")
    sp_count = lax.axis_size("sp")
    row_count, model_width = tokens.shape
    capacity = row_count // bag_count * 5 // 4
    slot_count = bag_count * capacity
    local_width = model_width // sp_count
    key_count = sp_count * slot_count
    bag_of = row_seq // SEQ_BAG
    member = (bag_of[:, None] == jnp.arange(bag_count, dtype=jnp.int32)[None, :]).astype(jnp.int32)
    before = jnp.cumsum(member, axis=0) - member
    rank_in = jnp.sum(before * member, axis=1)
    position = bag_of * capacity + rank_in
    source_row = (
        jnp.zeros((slot_count,), jnp.int32).at[position].set(jnp.arange(row_count, dtype=jnp.int32))
    )
    filled = jnp.zeros((slot_count,), jnp.bool_).at[position].set(True)
    slot_seq = jnp.where(filled, jnp.take(row_seq, source_row), -1)
    send_rows = jnp.where(
        filled[:, None], jnp.take(tokens, source_row, axis=0), jnp.zeros((), jnp.bfloat16)
    )
    arrived, arrived_seq = (
        lax.all_to_all(send_rows, "bag", split_axis=0, concat_axis=0, tiled=True),
        lax.all_to_all(
            slot_seq.astype(jnp.bfloat16), "bag", split_axis=0, concat_axis=0, tiled=True
        ),
    )
    mods = lookup(arrived_seq.astype(jnp.int32), modulation)
    packed = project(arrived, mods, w_qkv).reshape(slot_count, 3, sp_count, local_width)
    code_copies = jnp.broadcast_to(arrived_seq[:, None, None, None], (slot_count, 1, sp_count, 1))
    by_head, head_seq = (
        lax.all_to_all(packed, "sp", split_axis=2, concat_axis=0, tiled=True),
        lax.all_to_all(code_copies, "sp", split_axis=2, concat_axis=0, tiled=True),
    )
    attended = attend(
        by_head.reshape(key_count, 3, local_width), head_seq.reshape(key_count).astype(jnp.int32)
    )
    by_slot = lax.all_to_all(
        attended.reshape(key_count, 1, local_width), "sp", split_axis=0, concat_axis=1, tiled=True
    )
    finished = finish(arrived, by_slot.reshape(slot_count, model_width), mods, w_out, w_fc1, w_fc2)
    returned = lax.all_to_all(finished, "bag", split_axis=0, concat_axis=0, tiled=True)
    return jnp.take(returned, position, axis=0)


def solution(mesh):
    placed = (P(("bag", "sp"), None), P(("bag", "sp")), P(), P(), P(), P(), P())
    return jax.shard_map(
        shards, mesh=mesh, in_specs=placed, out_specs=P(("bag", "sp"), None), check_vma=False
    )
```

profile of v0, /device:TPU:0, one launch (start us, length us, event | category | flops | bytes accessed | tf_op | source)
XLA Modules:
  0.0 309.8 jit_solution(6032710517958751895)
XLA Ops:
  0.0 0.8 compare_convert_fusion
  0.8 1.2 reduce-window.6
  2.4 0.7 fusion.65
  3.1 0.7 compare_and_fusion.1
  3.8 1.4 scatter_custom_fusion.1
  5.3 3.6 %gather_fusion.1 = s32[320]{0:T(512)S(1)} fusion(s32[256]{0:T(256)} %param.10, s32[1024]{0:T(1024)S(1)} %pad_clamp_fusion.1), kind=kCustom, calls=%fused_computation.1 | custom fusion | bytes 3840 | tf_op jit(solution)/shard_map/jit(_take)/gather | solution.py:101
  8.9 1.5 scatter_custom_fusion
  11.1 4.2 %all-to-all-start.1 = ((bf16[4,80,1]{1,2,0:T(2,128)(2,1)}), bf16[4,80,1]{1,2,0:T(2,128)(2,1)S(1)}, u32[]{:S(2)}, u32[]{:S(2)}) async-start(bf16[4,80,1]{1,2,0:T(2,128)(2,1)} %all_to_all.63), calls=%async_computation.1 | async-start | bytes 4096 | tf_op jit(solution)/shard_map/all_to_all | solution.py:107
  15.5 2.7 gather_fusion
  18.2 2.3 select_select_fusion
  20.5 3.5 %all-to-all-start = ((bf16[4,80,1152]{2,1,0:T(8,128)(2,1)}), bf16[4,80,1152]{2,1,0:T(8,128)(2,1)S(1)}, u32[]{:S(2)}, u32[]{:S(2)}) async-start(bf16[4,80,1152]{2,1,0:T(8,128)(2,1)} %select_select_fusion), calls=%async_computation | async-start | bytes 1474560 | tf_op jit(solution)/shard_map/all_to_all | solution.py:106
  25.3 0.7 reshape.218
  26.0 6.2 %fusion.59 = f32[320,6,1152]{2,0,1:T(8,128)} fusion(f32[4,6,1152]{2,0,1:T(4,128)S(1)} %copy-done.5, s32[320]{0:T(512)S(1)} %convert_element_type.74), kind=kOutput, calls=%fused_computation.68 | convolution fusion | flops 106169600 | bytes 8959232 | tf_op jit(solution)/shard_map/dot_general | solution.py:24
  32.2 2.9 all-to-all-done
  35.0 6.3 %all-to-all-start.2 = ((bf16[8,2,160]{2,1,0:T(2,128)(2,1)}), bf16[8,2,160]{2,1,0:T(2,128)(2,1)S(1)}, u32[]{:S(2)}, u32[]{:S(2)}) async-start(bf16[8,2,160]{2,1,0:T(2,128)(2,1)} %reshape.218), calls=%async_computation.2 | async-start | bytes 16384 | tf_op jit(solution)/shard_map/all_to_all | solution.py:116
  42.1 2.2 fusion.39
  44.3 7.7 %convolution_convert_fusion = bf16[320,3456]{1,0:T(8,128)(2,1)} fusion(bf16[320,1152]{1,0:T(8,128)(2,1)S(1)} %fusion.39, bf16[1152,3456]{1,0:T(8,128)(2,1)} %param.12), kind=kOutput, calls=%fused_computation.22 | convolution fusion | flops 2549145600 | bytes 10911744 | tf_op jit(solution)/shard_map/dot_general | solution.py:34
  52.0 4.4 %copy.20 = bf16[320,3456]{0,1:T(8,128)(2,1)} copy(bf16[320,3456]{1,0:T(8,128)(2,1)} %convolution_convert_fusion) | data formatting | bytes 4423680 | tf_op jit(solution)/shard_map/convert_element_type | solution.py:34
  56.4 3.6 %copy.21 = bf16[320,3,8,144]{0,3,1,2:T(8,128)(2,1)} copy(bf16[320,3,8,144]{0,3,2,1:T(8,128)(2,1)} %bitcast.141) | data formatting | bytes 4423680 | tf_op jit(solution)/shard_map/reshape | solution.py:112
  60.0 6.0 %all-to-all-start.3 = ((bf16[320,3,8,144]{0,3,1,2:T(8,128)(2,1)}), bf16[320,3,8,144]{0,3,1,2:T(8,128)(2,1)}, u32[]{:S(2)}, u32[]{:S(2)}) async-start(bf16[320,3,8,144]{0,3,1,2:T(8,128)(2,1)} %copy.21), calls=%async_computation.3 | async-start | bytes 5308416 | tf_op jit(solution)/shard_map/all_to_all | solution.py:115
  66.2 59.2 %all-to-all-done.3 = bf16[320,3,8,144]{0,3,1,2:T(8,128)(2,1)} async-done(((bf16[320,3,8,144]{0,3,1,2:T(8,128)(2,1)}), bf16[320,3,8,144]{0,3,1,2:T(8,128)(2,1)}, u32[]{:S(2)}, u32[]{:S(2)}) %all-to-all-start.3) | async-done | bytes 2211872 | tf_op jit(solution)/shard_map/all_to_all | solution.py:115
  125.4 3.9 %copy.22 = bf16[8,320,3,1,144]{1,0,4,2,3:T(8,128)(2,1)} copy(bf16[8,320,3,1,144]{1,4,2,0,3:T(8,128)(2,1)} %bitcast.20) | data formatting | bytes 4423680 | tf_op jit(solution)/shard_map/all_to_all | solution.py:115
  129.4 5.2 %reshape.161 = bf16[2560,3,144]{0,2,1:T(8,128)(2,1)} reshape(bf16[8,320,3,1,144]{1,0,4,2,3:T(8,128)(2,1)} %copy.22) | data formatting | bytes 4423680 | tf_op jit(solution)/shard_map/reshape | solution.py:119
  134.6 3.0 fusion.76
  137.6 68.0 %while.10 = (s32[]{:T(128)}, bf16[5,512,144]{1,2,0:T(8,128)(2,1)}, s32[5]{0:T(128)S(1)}, s32[2560]{0:T(1024)S(1)}, bf16[2560,2,72]{0,2,1:T(8,128)(2,1)}, /*index...) while((s32[]{:T(128)}, bf16[5,512,144]{1,2,0:T(8,128)(2,1)}, ...), condition=%wide.region_10.11_spmd, body=%wide.region_7.10_spmd.sunk | while | flops 785266688 | bytes 38802096 | solution.py:65
  138.9 0.8 broadcast_compare_fusion.2
  139.7 3.7 %fusion.95 = (f32[2,512]{1,0:T(2,128)S(1)}, f32[2,512,2560]{2,1,0:T(8,128)S(1)}) fusion(pred[512,2560]{1,0:T(8,128)(4,1)S(1)} %broadcast_compare_fusion.2, bf16[2560,2,72]{0,2,1:T(8,128)(2,1)} %get-tuple-element.142, bf16[2560,2,72]{0,2,1:T(8,128)(2,1)} %get-tuple-element.141, s32[]{:T(128)S(6)} %select_n.87), kind=kOutput, calls=%fused_computation.7.clone.1 | convolution fusion | flops 385350656 | bytes 12685316 | tf_op jit(solution)/shard_map/while/body/eval_jaxpr/qhd,khd->hqk/dot_general | solution.py:52
  143.4 3.0 fusion.96
  146.4 4.1 %fusion.97 = bf16[512,2,72]{0,2,1:T(8,128)(2,1)S(1)} fusion(bf16[2560,2,72]{0,2,1:T(8,128)(2,1)} %get-tuple-element.143, f32[2,512,2560]{2,1,0:T(8,128)S(1)} %get-tuple-element.113, f32[2,512]{1,0:T(2,128)S(1)} %get-tuple-element.114, pred[512,2560]{1,0:T(8,128)(4,1)S(1)} %broadcast_compare_fusion.2, f32[512,2]{0,1:T(2,128)S(1)} %bitcast.150), kind=kOutput, calls=%fused_computation.15.clone.1 | convolution fusion | flops 388120576 | bytes 12689408 | tf_op jit(solution)/shard_map/while/body/eval_jaxpr/hqk,khd->qhd/dot_general | solution.py:61
  150.5 0.7 constant_dynamic-update-slice_fusion.2
  152.5 0.8 broadcast_compare_fusion.2
  153.3 3.7 %fusion.95 = (f32[2,512]{1,0:T(2,128)S(1)}, f32[2,512,2560]{2,1,0:T(8,128)S(1)}) fusion(pred[512,2560]{1,0:T(8,128)(4,1)S(1)} %broadcast_compare_fusion.2, bf16[2560,2,72]{0,2,1:T(8,128)(2,1)} %get-tuple-element.142, bf16[2560,2,72]{0,2,1:T(8,128)(2,1)} %get-tuple-element.141, s32[]{:T(128)S(6)} %select_n.87), kind=kOutput, calls=%fused_computation.7.clone.1 | convolution fusion | flops 385350656 | bytes 12685316 | tf_op jit(solution)/shard_map/while/body/eval_jaxpr/qhd,khd->hqk/dot_general | solution.py:52
  157.0 3.0 fusion.96
  160.1 4.1 %fusion.97 = bf16[512,2,72]{0,2,1:T(8,128)(2,1)S(1)} fusion(bf16[2560,2,72]{0,2,1:T(8,128)(2,1)} %get-tuple-element.143, f32[2,512,2560]{2,1,0:T(8,128)S(1)} %get-tuple-element.113, f32[2,512]{1,0:T(2,128)S(1)} %get-tuple-element.114, pred[512,2560]{1,0:T(8,128)(4,1)S(1)} %broadcast_compare_fusion.2, f32[512,2]{0,1:T(2,128)S(1)} %bitcast.150), kind=kOutput, calls=%fused_computation.15.clone.1 | convolution fusion | flops 388120576 | bytes 12689408 | tf_op jit(solution)/shard_map/while/body/eval_jaxpr/hqk,khd->qhd/dot_general | solution.py:61
  164.1 0.7 constant_dynamic-update-slice_fusion.2
  166.1 0.8 broadcast_compare_fusion.2
  166.9 3.7 %fusion.95 = (f32[2,512]{1,0:T(2,128)S(1)}, f32[2,512,2560]{2,1,0:T(8,128)S(1)}) fusion(pred[512,2560]{1,0:T(8,128)(4,1)S(1)} %broadcast_compare_fusion.2, bf16[2560,2,72]{0,2,1:T(8,128)(2,1)} %get-tuple-element.142, bf16[2560,2,72]{0,2,1:T(8,128)(2,1)} %get-tuple-element.141, s32[]{:T(128)S(6)} %select_n.87), kind=kOutput, calls=%fused_computation.7.clone.1 | convolution fusion | flops 385350656 | bytes 12685316 | tf_op jit(solution)/shard_map/while/body/eval_jaxpr/qhd,khd->hqk/dot_general | solution.py:52
  170.6 3.0 fusion.96
  173.7 4.1 %fusion.97 = bf16[512,2,72]{0,2,1:T(8,128)(2,1)S(1)} fusion(bf16[2560,2,72]{0,2,1:T(8,128)(2,1)} %get-tuple-element.143, f32[2,512,2560]{2,1,0:T(8,128)S(1)} %get-tuple-element.113, f32[2,512]{1,0:T(2,128)S(1)} %get-tuple-element.114, pred[512,2560]{1,0:T(8,128)(4,1)S(1)} %broadcast_compare_fusion.2, f32[512,2]{0,1:T(2,128)S(1)} %bitcast.150), kind=kOutput, calls=%fused_computation.15.clone.1 | convolution fusion | flops 388120576 | bytes 12689408 | tf_op jit(solution)/shard_map/while/body/eval_jaxpr/hqk,khd->qhd/dot_general | solution.py:61
  177.7 0.7 constant_dynamic-update-slice_fusion.2
  179.7 0.8 broadcast_compare_fusion.2
  180.5 3.7 %fusion.95 = (f32[2,512]{1,0:T(2,128)S(1)}, f32[2,512,2560]{2,1,0:T(8,128)S(1)}) fusion(pred[512,2560]{1,0:T(8,128)(4,1)S(1)} %broadcast_compare_fusion.2, bf16[2560,2,72]{0,2,1:T(8,128)(2,1)} %get-tuple-element.142, bf16[2560,2,72]{0,2,1:T(8,128)(2,1)} %get-tuple-element.141, s32[]{:T(128)S(6)} %select_n.87), kind=kOutput, calls=%fused_computation.7.clone.1 | convolution fusion | flops 385350656 | bytes 12685316 | tf_op jit(solution)/shard_map/while/body/eval_jaxpr/qhd,khd->hqk/dot_general | solution.py:52
  184.2 3.0 fusion.96
  187.3 4.1 %fusion.97 = bf16[512,2,72]{0,2,1:T(8,128)(2,1)S(1)} fusion(bf16[2560,2,72]{0,2,1:T(8,128)(2,1)} %get-tuple-element.143, f32[2,512,2560]{2,1,0:T(8,128)S(1)} %get-tuple-element.113, f32[2,512]{1,0:T(2,128)S(1)} %get-tuple-element.114, pred[512,2560]{1,0:T(8,128)(4,1)S(1)} %broadcast_compare_fusion.2, f32[512,2]{0,1:T(2,128)S(1)} %bitcast.150), kind=kOutput, calls=%fused_computation.15.clone.1 | convolution fusion | flops 388120576 | bytes 12689408 | tf_op jit(solution)/shard_map/while/body/eval_jaxpr/hqk,khd->qhd/dot_general | solution.py:61
  193.3 0.8 broadcast_compare_fusion.2
  194.1 3.7 %fusion.95 = (f32[2,512]{1,0:T(2,128)S(1)}, f32[2,512,2560]{2,1,0:T(8,128)S(1)}) fusion(pred[512,2560]{1,0:T(8,128)(4,1)S(1)} %broadcast_compare_fusion.2, bf16[2560,2,72]{0,2,1:T(8,128)(2,1)} %get-tuple-element.142, bf16[2560,2,72]{0,2,1:T(8,128)(2,1)} %get-tuple-element.141, s32[]{:T(128)S(6)} %select_n.87), kind=kOutput, calls=%fused_computation.7.clone.1 | convolution fusion | flops 385350656 | bytes 12685316 | tf_op jit(solution)/shard_map/while/body/eval_jaxpr/qhd,khd->hqk/dot_general | solution.py:52
  197.8 3.0 fusion.96
  200.9 4.1 %fusion.97 = bf16[512,2,72]{0,2,1:T(8,128)(2,1)S(1)} fusion(bf16[2560,2,72]{0,2,1:T(8,128)(2,1)} %get-tuple-element.143, f32[2,512,2560]{2,1,0:T(8,128)S(1)} %get-tuple-element.113, f32[2,512]{1,0:T(2,128)S(1)} %get-tuple-element.114, pred[512,2560]{1,0:T(8,128)(4,1)S(1)} %broadcast_compare_fusion.2, f32[512,2]{0,1:T(2,128)S(1)} %bitcast.150), kind=kOutput, calls=%fused_computation.15.clone.1 | convolution fusion | flops 388120576 | bytes 12689408 | tf_op jit(solution)/shard_map/while/body/eval_jaxpr/hqk,khd->qhd/dot_general | solution.py:61
  205.6 2.3 copy.27
  207.9 8.5 %reshape.212 = bf16[2560,1,144]{2,1,0:T(2,128)(2,1)} reshape(bf16[5,512,144]{2,1,0:T(8,128)(2,1)} %copy.27) | data formatting | bytes 1474560 | tf_op jit(solution)/shard_map/reshape;reshape | solution.py:122
  216.5 16.4 %reduce.4 = bf16[2560,144]{1,0:T(8,128)(2,1)} reduce(bf16[2560,1,144]{2,1,0:T(2,128)(2,1)} %reshape.212, bf16[]{:T(256)} %broadcast.160), dimensions={1}, to_apply=%reshape.212.reduce_sub_computation | reduce | bytes 1474562 | tf_op jit(solution)/shard_map/reshape;reshape | solution.py:122
  232.9 4.4 %reshape.220 = bf16[8,2,23040]{2,1,0:T(2,128)(2,1)} reshape(bf16[2560,144]{1,0:T(8,128)(2,1)} %reduce.4) | data formatting | bytes 1474560
  237.3 22.9 %all_to_all.70 = bf16[8,2,23040]{2,1,0:T(2,128)(2,1)S(1)} all-to-all(bf16[8,2,23040]{2,1,0:T(2,128)(2,1)} %reshape.220), channel_id=1, replica_groups=mesh['bag'=4,'sp'=8] {'sp'}, dimensions={0} | all-to-all | bytes 1474560 | tf_op jit(solution)/shard_map/all_to_all | solution.py:121
  260.2 5.3 %reshape.221 = bf16[2560,1,144]{2,1,0:T(2,128)(2,1)} reshape(bf16[8,2,23040]{2,1,0:T(2,128)(2,1)S(1)} %all_to_all.70) | data formatting | bytes 1474560
  265.6 6.1 %copy.25 = bf16[2560,1,144]{0,2,1:T(8,128)(2,1)} copy(bf16[2560,1,144]{2,1,0:T(2,128)(2,1)} %reshape.221) | data formatting | bytes 1474560 | tf_op jit(solution)/shard_map/all_to_all | solution.py:121
  271.6 2.5 all_to_all.58
  274.2 1.3 copy.26
  275.5 2.8 fusion.77
  278.3 1.2 copy-done.4
  279.8 11.4 %fusion.30 = bf16[320,1152]{1,0:T(8,128)(2,1)} fusion(f32[320,1152]{1,0:T(8,128)} %copy-done.4, bf16[2304,1152]{1,0:T(8,128)(2,1)} %param.15, f32[320,6,1152]{2,0,1:T(8,128)} %fusion.59, bf16[1152,2304]{1,0:T(8,128)(2,1)} %param.14, f32[320]{0:T(512)S(1)} %add_rsqrt_fusion, f32[320]{0:T(512)S(1)} %broadcast_multiply_fusion), kind=kOutput, calls=%fused_computation.36 | convolution fusion | flops 3407339520 | bytes 18729472 | tf_op jit(solution)/shard_map/dot_general | solution.py:80
  291.1 3.5 %all-to-all-start.5 = ((bf16[4,80,1152]{2,1,0:T(8,128)(2,1)}), bf16[4,80,1152]{2,1,0:T(8,128)(2,1)S(1)}, u32[]{:S(2)}, u32[]{:S(2)}) async-start(bf16[4,80,1152]{2,1,0:T(8,128)(2,1)} %bitcast.149), calls=%async_computation.5 | async-start | bytes 1474560 | tf_op jit(solution)/shard_map/all_to_all | solution.py:125
  294.6 11.0 %all-to-all-done.5 = bf16[4,80,1152]{2,1,0:T(8,128)(2,1)S(1)} async-done(((bf16[4,80,1152]{2,1,0:T(8,128)(2,1)}), bf16[4,80,1152]{2,1,0:T(8,128)(2,1)S(1)}, u32[]{:S(2)}, u32[]{:S(2)}) %all-to-all-start.5) | async-done | bytes 737312 | tf_op jit(solution)/shard_map/all_to_all | solution.py:125
  305.7 2.1 gather_fusion.2
  307.8 2.0 broadcast_select_fusion
  (60 shorter events, 8.6 us)
Async XLA Ops:
  0.0 275.4 %copy-start = (bf16[1152,1152]{1,0:T(8,128)(2,1)S(1)}, bf16[1152,1152]{1,0:T(8,128)(2,1)}, u32[]{:S(2)}) copy-start(bf16[1152,1152]{1,0:T(8,128)(2,1)} %param.13) | copy-start | bytes 7962628
  0.0 15.5 %copy-start.1 = (bf16[256,1152]{1,0:T(8,128)(2,1)S(1)}, bf16[256,1152]{1,0:T(8,128)(2,1)}, u32[]{:S(2)}) copy-start(bf16[256,1152]{1,0:T(8,128)(2,1)} %param.9) | copy-start | bytes 1769476
  11.1 9.4 %all-to-all-start.1 = ((bf16[4,80,1]{1,2,0:T(2,128)(2,1)}), bf16[4,80,1]{1,2,0:T(2,128)(2,1)S(1)}, u32[]{:S(2)}, u32[]{:S(2)}) async-start(bf16[4,80,1]{1,2,0:T(2,128)(2,1)} %all_to_all.63), calls=%async_computation.1 | async-start | bytes 4096 | tf_op jit(solution)/shard_map/all_to_all | solution.py:107
  18.2 7.8 %copy-start.5 = (f32[4,6,1152]{2,0,1:T(4,128)S(1)}, f32[4,6,1152]{2,0,1:T(4,128)}, u32[]{:S(2)}) copy-start(f32[4,6,1152]{2,0,1:T(4,128)} %param.11) | copy-start | bytes 331780
  20.5 14.6 %all-to-all-start = ((bf16[4,80,1152]{2,1,0:T(8,128)(2,1)}), bf16[4,80,1152]{2,1,0:T(8,128)(2,1)S(1)}, u32[]{:S(2)}, u32[]{:S(2)}) async-start(bf16[4,80,1152]{2,1,0:T(8,128)(2,1)} %select_select_fusion), calls=%async_computation | async-start | bytes 1474560 | tf_op jit(solution)/shard_map/all_to_all | solution.py:106
  35.0 9.3 %copy-start.2 = (bf16[4,80,1152]{2,1,0:T(8,128)(2,1)}, bf16[4,80,1152]{2,1,0:T(8,128)(2,1)S(1)}, u32[]{:S(2)}) copy-start(bf16[4,80,1152]{2,1,0:T(8,128)(2,1)S(1)} %all-to-all-done) | copy-start | bytes 2211844
  35.0 25.0 %all-to-all-start.2 = ((bf16[8,2,160]{2,1,0:T(2,128)(2,1)}), bf16[8,2,160]{2,1,0:T(2,128)(2,1)S(1)}, u32[]{:S(2)}, u32[]{:S(2)}) async-start(bf16[8,2,160]{2,1,0:T(2,128)(2,1)} %reshape.218), calls=%async_computation.2 | async-start | bytes 16384 | tf_op jit(solution)/shard_map/all_to_all | solution.py:116
  60.0 65.4 %all-to-all-start.3 = ((bf16[320,3,8,144]{0,3,1,2:T(8,128)(2,1)}), bf16[320,3,8,144]{0,3,1,2:T(8,128)(2,1)}, u32[]{:S(2)}, u32[]{:S(2)}) async-start(bf16[320,3,8,144]{0,3,1,2:T(8,128)(2,1)} %copy.21), calls=%async_computation.3 | async-start | bytes 5308416 | tf_op jit(solution)/shard_map/all_to_all | solution.py:115
  265.6 9.9 %copy-start.3 = (bf16[4,80,1152]{2,1,0:T(8,128)(2,1)S(1)}, bf16[4,80,1152]{2,1,0:T(8,128)(2,1)}, u32[]{:S(2)}) copy-start(bf16[4,80,1152]{2,1,0:T(8,128)(2,1)} %copy-done.2) | copy-start | bytes 2211844
  278.3 1.2 copy-start.4
  291.1 14.6 %all-to-all-start.5 = ((bf16[4,80,1152]{2,1,0:T(8,128)(2,1)}), bf16[4,80,1152]{2,1,0:T(8,128)(2,1)S(1)}, u32[]{:S(2)}, u32[]{:S(2)}) async-start(bf16[4,80,1152]{2,1,0:T(8,128)(2,1)} %bitcast.149), calls=%async_computation.5 | async-start | bytes 1474560 | tf_op jit(solution)/shard_map/all_to_all | solution.py:125
where the time goes:
time: 312 us; the launch traced here: 310 us
  waiting for transfers between devices  73.2 us (23%)
  local copies, waits for them, and re-layouts  72.6 us (23%)
  matrix products  66.9 us (21%)
  other arithmetic  47.3 us (15%)
  starting transfers between devices  23.5 us (8%)
  blocking collectives  22.9 us (7%)
  loops' own time  3.18 us (1%)
    all_to_all x1, waiting for transfers between devices, shards(): lax.all_to_all(packed, 'sp', split_axis=2, concat_axis=0, tiled=True)  59.2 us
    all_to_all x1, blocking collectives, shards(): lax.all_to_all(attended.reshape(key_count, 1, local_width), 'sp', split_a...  22.9 us
    dot_general x5, matrix products, one_block(): jnp.einsum('hqk,khd->qhd', probs, values, preferred_element_type=jnp.floa...  20.3 us
    dot_general x5, matrix products, one_block(): jnp.einsum('qhd,khd->hqk', query_part, key_rows, preferred_element_type=j...  18.6 us
    another operation x1, other arithmetic, shards(): attended.reshape(key_count, 1, local_width)  16.4 us
    reduce_sum x5, other arithmetic, one_block(): denominator = jnp.sum(raised, axis=-1)  15.2 us
    unnamed x18, local copies, waits for them, and re-layouts  12.2 us
    dot_general x1, matrix products, finish(): jnp.dot(active, w_fc2, preferred_element_type=jnp.float32)  11.4 us
  transfers between devices with their start and end apart: 5, of which 3 were waited for; matrix products, arithmetic and copies ran while one was open for 10% of the time, Pallas kernels for 0%

commit v1 on v0

--- a/solution.py
+++ b/solution.py
@@ -3,6 +3,7 @@
 import jax.numpy as jnp
 from jax import lax
 from jax.sharding import PartitionSpec as P
+from jax.lax import all_to_all, axis_size
 
 HD = 72
 SEQ_BAG = 1
@@ -82,6 +83,14 @@
 
 
 def shards(tokens, row_seq, modulation, w_qkv, w_out, w_fc1, w_fc2):
+
+    def lead_members_all_all(point, peer_axis):
+        left_arr = jnp.concatenate(
+            all_to_all(jnp.stack(jnp.split(point, axis_size(peer_axis), axis=0)), peer_axis, 0, 0),
+            axis=1,
+        )
+        return left_arr
+
     bag_count = lax.axis_size("bag")
     sp_count = lax.axis_size("sp")
     row_count, model_width = tokens.shape
@@ -118,9 +127,7 @@
     attended = attend(
         by_head.reshape(key_count, 3, local_width), head_seq.reshape(key_count).astype(jnp.int32)
     )
-    by_slot = lax.all_to_all(
-        attended.reshape(key_count, 1, local_width), "sp", split_axis=0, concat_axis=1, tiled=True
-    )
+    by_slot = lead_members_all_all(attended.reshape(key_count, 1, local_width), "sp")
     finished = finish(arrived, by_slot.reshape(slot_count, model_width), mods, w_out, w_fc1, w_fc2)
     returned = lax.all_to_all(finished, "bag", split_axis=0, concat_axis=0, tiled=True)
     return jnp.take(returned, position, axis=0)

time: 312 us -> 281 us (0.901)
  local copies, waits for them, and re-layouts: 72.6 us -> 55.4 us
  other arithmetic: 47.3 us -> 30.9 us
  blocking collectives: 22.9 us -> 26.3 us
    another operation x3 -> x2, other arithmetic: 17.7 us -> 1.24 us  [the longest x1 16.4 us: shards(): attended.reshape(key_count, 1, local_width)]
    all_to_all x3 -> x0, local copies, waits for them, and re-layouts: 9.86 us -> none  [shards(): lax.all_to_all(attended.reshape(key_count, 1, local_width), 'sp', split_a...]
    another operation x2 -> x1, local copies, waits for them, and re-layouts: 10.9 us -> 2.83 us  [shards(): attended.reshape(key_count, 1, local_width)]
    all_to_all x1, blocking collectives: 22.9 us -> 26.3 us  [lead_members_all_all(): all_to_all(jnp.stack(jnp.split(point, axis_size(peer_axis), axis=0)), pee...]
    unnamed x18 -> x23, local copies, waits for them, and re-layouts: 12.2 us -> 9.19 us
  transfers between devices with their start and end apart: 5 -> 5, of which waited for: 3 -> 3; matrix products, arithmetic and copies ran while one was open for 10% -> 11% of each run, Pallas kernels for 0% -> 0%
where the time goes in v1:
time: 281 us; the launch traced here: 279 us
  waiting for transfers between devices  73.1 us (26%)
  matrix products  66.9 us (24%)
  local copies, waits for them, and re-layouts  55.4 us (20%)
  other arithmetic  30.9 us (11%)
  blocking collectives  26.3 us (9%)
  starting transfers between devices  23.5 us (8%)
  loops' own time  3.18 us (1%)
    all_to_all x1, waiting for transfers between devices, shards(): lax.all_to_all(packed, 'sp', split_axis=2, concat_axis=0, tiled=True)  59.2 us
    all_to_all x1, blocking collectives, lead_members_all_all(): all_to_all(jnp.stack(jnp.split(point, axis_size(peer_axis), axis=0)), pee...  26.3 us
    dot_general x5, matrix products, one_block(): jnp.einsum('hqk,khd->qhd', probs, values, preferred_element_type=jnp.floa...  20.3 us
    dot_general x5, matrix products, one_block(): jnp.einsum('qhd,khd->hqk', query_part, key_rows, preferred_element_type=j...  18.6 us
    reduce_sum x5, other arithmetic, one_block(): denominator = jnp.sum(raised, axis=-1)  15.2 us
    dot_general x1, matrix products, finish(): jnp.dot(active, w_fc2, preferred_element_type=jnp.float32)  11.4 us
    all_to_all x1, waiting for transfers between devices, shards(): lax.all_to_all(finished, 'bag', split_axis=0, concat_axis=0, tiled=True)  11 us
    unnamed x23, local copies, waits for them, and re-layouts  9.19 us
  transfers between devices with their start and end apart: 5, of which 3 were waited for; matrix products, arithmetic and copies ran while one was open for 11% of the time, Pallas kernels for 0%

profile of v1, /device:TPU:0, one launch (start us, length us, event | category | flops | bytes accessed | tf_op | source)
XLA Modules:
  0.0 279.5 jit_solution(6469937358615033665)
XLA Ops:
  0.0 0.8 compare_convert_fusion
  0.8 1.2 reduce-window.6
  2.4 0.7 fusion.73
  3.1 0.7 compare_and_fusion.1
  3.8 1.4 scatter_custom_fusion.1
  5.3 3.6 %gather_fusion.1 = s32[320]{0:T(512)S(1)} fusion(s32[256]{0:T(256)} %param.10, s32[1024]{0:T(1024)S(1)} %pad_clamp_fusion.1), kind=kCustom, calls=%fused_computation.1 | custom fusion | bytes 3840 | tf_op jit(solution)/shard_map/jit(_take)/gather | solution.py:110
  8.9 1.5 scatter_custom_fusion
  11.1 4.2 %all-to-all-start.1 = ((bf16[4,80,1]{1,2,0:T(2,128)(2,1)}), bf16[4,80,1]{1,2,0:T(2,128)(2,1)S(1)}, u32[]{:S(2)}, u32[]{:S(2)}) async-start(bf16[4,80,1]{1,2,0:T(2,128)(2,1)} %all_to_all.53), calls=%async_computation.1 | async-start | bytes 4096 | tf_op jit(solution)/shard_map/all_to_all | solution.py:116
  15.5 2.7 gather_fusion
  18.2 2.3 select_select_fusion
  20.5 3.5 %all-to-all-start = ((bf16[4,80,1152]{2,1,0:T(8,128)(2,1)}), bf16[4,80,1152]{2,1,0:T(8,128)(2,1)S(1)}, u32[]{:S(2)}, u32[]{:S(2)}) async-start(bf16[4,80,1152]{2,1,0:T(8,128)(2,1)} %select_select_fusion), calls=%async_computation | async-start | bytes 1474560 | tf_op jit(solution)/shard_map/all_to_all | solution.py:115
  24.6 0.7 reduce.3
  26.0 6.2 %fusion.67 = f32[320,6,1152]{2,0,1:T(8,128)} fusion(f32[4,6,1152]{2,0,1:T(4,128)S(1)} %copy-done.5, s32[320]{0:T(512)S(1)} %convert_element_type.74), kind=kOutput, calls=%fused_computation.84 | convolution fusion | flops 106169600 | bytes 8959232 | tf_op jit(solution)/shard_map/dot_general | solution.py:25
  32.2 2.8 %all-to-all-done = bf16[4,80,1152]{2,1,0:T(8,128)(2,1)S(1)} async-done(((bf16[4,80,1152]{2,1,0:T(8,128)(2,1)}), bf16[4,80,1152]{2,1,0:T(8,128)(2,1)S(1)}, u32[]{:S(2)}, u32[]{:S(2)}) %all-to-all-start) | async-done | bytes 737312 | tf_op jit(solution)/shard_map/all_to_all | solution.py:115
  35.0 6.3 %all-to-all-start.2 = ((bf16[8,2,160]{2,1,0:T(2,128)(2,1)}), bf16[8,2,160]{2,1,0:T(2,128)(2,1)S(1)}, u32[]{:S(2)}, u32[]{:S(2)}) async-start(bf16[8,2,160]{2,1,0:T(2,128)(2,1)} %reshape.216), calls=%async_computation.2 | async-start | bytes 16384 | tf_op jit(solution)/shard_map/all_to_all | solution.py:125
  42.1 2.2 fusion.39
  44.3 7.7 %convolution_convert_fusion = bf16[320,3456]{1,0:T(8,128)(2,1)} fusion(bf16[320,1152]{1,0:T(8,128)(2,1)S(1)} %fusion.39, bf16[1152,3456]{1,0:T(8,128)(2,1)} %param.12), kind=kOutput, calls=%fused_computation.22 | convolution fusion | flops 2549145600 | bytes 10911744 | tf_op jit(solution)/shard_map/dot_general | solution.py:35
  52.0 4.4 %copy.26 = bf16[320,3456]{0,1:T(8,128)(2,1)} copy(bf16[320,3456]{1,0:T(8,128)(2,1)} %convolution_convert_fusion) | data formatting | bytes 4423680 | tf_op jit(solution)/shard_map/convert_element_type | solution.py:35
  56.4 3.6 %copy.27 = bf16[320,3,8,144]{0,3,1,2:T(8,128)(2,1)} copy(bf16[320,3,8,144]{0,3,2,1:T(8,128)(2,1)} %bitcast.174) | data formatting | bytes 4423680 | tf_op jit(solution)/shard_map/reshape | solution.py:121
  60.0 6.0 %all-to-all-start.3 = ((bf16[320,3,8,144]{0,3,1,2:T(8,128)(2,1)}), bf16[320,3,8,144]{0,3,1,2:T(8,128)(2,1)}, u32[]{:S(2)}, u32[]{:S(2)}) async-start(bf16[320,3,8,144]{0,3,1,2:T(8,128)(2,1)} %copy.27), calls=%async_computation.3 | async-start | bytes 5308416 | tf_op jit(solution)/shard_map/all_to_all | solution.py:124
  66.2 59.2 %all-to-all-done.3 = bf16[320,3,8,144]{0,3,1,2:T(8,128)(2,1)} async-done(((bf16[320,3,8,144]{0,3,1,2:T(8,128)(2,1)}), bf16[320,3,8,144]{0,3,1,2:T(8,128)(2,1)}, u32[]{:S(2)}, u32[]{:S(2)}) %all-to-all-start.3) | async-done | bytes 2211872 | tf_op jit(solution)/shard_map/all_to_all | solution.py:124
  125.4 3.9 %copy.28 = bf16[8,320,3,1,144]{1,0,4,2,3:T(8,128)(2,1)} copy(bf16[8,320,3,1,144]{1,4,2,0,3:T(8,128)(2,1)} %bitcast.20) | data formatting | bytes 4423680 | tf_op jit(solution)/shard_map/all_to_all | solution.py:124
  129.4 5.2 %reshape.160 = bf16[2560,3,144]{0,2,1:T(8,128)(2,1)} reshape(bf16[8,320,3,1,144]{1,0,4,2,3:T(8,128)(2,1)} %copy.28) | data formatting | bytes 4423680 | tf_op jit(solution)/shard_map/reshape | solution.py:128
  134.6 3.0 %fusion.84 = (bf16[2560,1,144]{0,2,1:T(8,128)(2,1)}, bf16[2560,1,144]{0,2,1:T(8,128)(2,1)}, bf16[2560,1,144]{0,2,1:T(8,128)(2,1)}) fusion(bf16[2560,3,144]{0,2,1:T(8,128)(2,1)} %reshape.160), kind=kLoop, calls=%fused_computation.116 | loop fusion | bytes 4423680 | tf_op jit(solution)/shard_map/slice | solution.py:44
  137.6 68.0 %while.10 = (s32[]{:T(128)}, bf16[5,512,144]{1,2,0:T(8,128)(2,1)}, s32[5]{0:T(128)S(1)}, s32[2560]{0:T(1024)S(1)}, bf16[2560,2,72]{0,2,1:T(8,128)(2,1)}, /*index...) while((s32[]{:T(128)}, bf16[5,512,144]{1,2,0:T(8,128)(2,1)}, ...), condition=%wide.region_10.11_spmd, body=%wide.region_7.10_spmd.sunk | while | flops 785266688 | bytes 38802096 | solution.py:66
  138.9 0.8 broadcast_compare_fusion.2
  139.7 3.7 %fusion.103 = (f32[2,512]{1,0:T(2,128)S(1)}, f32[2,512,2560]{2,1,0:T(8,128)S(1)}) fusion(pred[512,2560]{1,0:T(8,128)(4,1)S(1)} %broadcast_compare_fusion.2, bf16[2560,2,72]{0,2,1:T(8,128)(2,1)} %get-tuple-element.142, bf16[2560,2,72]{0,2,1:T(8,128)(2,1)} %get-tuple-element.141, s32[]{:T(128)S(6)} %select_n.87), kind=kOutput, calls=%fused_computation.7.clone.1 | convolution fusion | flops 385350656 | bytes 12685316 | tf_op jit(solution)/shard_map/while/body/eval_jaxpr/qhd,khd->hqk/dot_general | solution.py:53
  143.4 3.0 %fusion.104 = f32[2,512]{1,0:T(2,128)S(1)} fusion(f32[2,512,2560]{2,1,0:T(8,128)S(1)} %get-tuple-element.113, f32[2,512]{1,0:T(2,128)S(1)} %get-tuple-element.114, pred[512,2560]{1,0:T(8,128)(4,1)S(1)} %broadcast_compare_fusion.2), kind=kLoop, calls=%fused_computation.8.clone.1 | loop fusion | flops 10484736 | bytes 11804672 | tf_op jit(solution)/shard_map/while/body/eval_jaxpr/reduce_sum | solution.py:60
  146.4 4.1 %fusion.105 = bf16[512,2,72]{0,2,1:T(8,128)(2,1)S(1)} fusion(bf16[2560,2,72]{0,2,1:T(8,128)(2,1)} %get-tuple-element.143, f32[2,512,2560]{2,1,0:T(8,128)S(1)} %get-tuple-element.113, f32[2,512]{1,0:T(2,128)S(1)} %get-tuple-element.114, pred[512,2560]{1,0:T(8,128)(4,1)S(1)} %broadcast_compare_fusion.2, f32[512,2]{0,1:T(2,128)S(1)} %bitcast.182), kind=kOutput, calls=%fused_computation.15.clone.1 | convolution fusion | flops 388120576 | bytes 12689408 | tf_op jit(solution)/shard_map/while/body/eval_jaxpr/hqk,khd->qhd/dot_general | solution.py:62
  150.5 0.7 constant_dynamic-update-slice_fusion.2
  152.5 0.8 broadcast_compare_fusion.2
  153.3 3.7 %fusion.103 = (f32[2,512]{1,0:T(2,128)S(1)}, f32[2,512,2560]{2,1,0:T(8,128)S(1)}) fusion(pred[512,2560]{1,0:T(8,128)(4,1)S(1)} %broadcast_compare_fusion.2, bf16[2560,2,72]{0,2,1:T(8,128)(2,1)} %get-tuple-element.142, bf16[2560,2,72]{0,2,1:T(8,128)(2,1)} %get-tuple-element.141, s32[]{:T(128)S(6)} %select_n.87), kind=kOutput, calls=%fused_computation.7.clone.1 | convolution fusion | flops 385350656 | bytes 12685316 | tf_op jit(solution)/shard_map/while/body/eval_jaxpr/qhd,khd->hqk/dot_general | solution.py:53
  157.0 3.0 %fusion.104 = f32[2,512]{1,0:T(2,128)S(1)} fusion(f32[2,512,2560]{2,1,0:T(8,128)S(1)} %get-tuple-element.113, f32[2,512]{1,0:T(2,128)S(1)} %get-tuple-element.114, pred[512,2560]{1,0:T(8,128)(4,1)S(1)} %broadcast_compare_fusion.2), kind=kLoop, calls=%fused_computation.8.clone.1 | loop fusion | flops 10484736 | bytes 11804672 | tf_op jit(solution)/shard_map/while/body/eval_jaxpr/reduce_sum | solution.py:60
  160.1 4.1 %fusion.105 = bf16[512,2,72]{0,2,1:T(8,128)(2,1)S(1)} fusion(bf16[2560,2,72]{0,2,1:T(8,128)(2,1)} %get-tuple-element.143, f32[2,512,2560]{2,1,0:T(8,128)S(1)} %get-tuple-element.113, f32[2,512]{1,0:T(2,128)S(1)} %get-tuple-element.114, pred[512,2560]{1,0:T(8,128)(4,1)S(1)} %broadcast_compare_fusion.2, f32[512,2]{0,1:T(2,128)S(1)} %bitcast.182), kind=kOutput, calls=%fused_computation.15.clone.1 | convolution fusion | flops 388120576 | bytes 12689408 | tf_op jit(solution)/shard_map/while/body/eval_jaxpr/hqk,khd->qhd/dot_general | solution.py:62
  166.1 0.8 broadcast_compare_fusion.2
  166.9 3.7 %fusion.103 = (f32[2,512]{1,0:T(2,128)S(1)}, f32[2,512,2560]{2,1,0:T(8,128)S(1)}) fusion(pred[512,2560]{1,0:T(8,128)(4,1)S(1)} %broadcast_compare_fusion.2, bf16[2560,2,72]{0,2,1:T(8,128)(2,1)} %get-tuple-element.142, bf16[2560,2,72]{0,2,1:T(8,128)(2,1)} %get-tuple-element.141, s32[]{:T(128)S(6)} %select_n.87), kind=kOutput, calls=%fused_computation.7.clone.1 | convolution fusion | flops 385350656 | bytes 12685316 | tf_op jit(solution)/shard_map/while/body/eval_jaxpr/qhd,khd->hqk/dot_general | solution.py:53
  170.6 3.0 %fusion.104 = f32[2,512]{1,0:T(2,128)S(1)} fusion(f32[2,512,2560]{2,1,0:T(8,128)S(1)} %get-tuple-element.113, f32[2,512]{1,0:T(2,128)S(1)} %get-tuple-element.114, pred[512,2560]{1,0:T(8,128)(4,1)S(1)} %broadcast_compare_fusion.2), kind=kLoop, calls=%fused_computation.8.clone.1 | loop fusion | flops 10484736 | bytes 11804672 | tf_op jit(solution)/shard_map/while/body/eval_jaxpr/reduce_sum | solution.py:60
  173.7 4.1 %fusion.105 = bf16[512,2,72]{0,2,1:T(8,128)(2,1)S(1)} fusion(bf16[2560,2,72]{0,2,1:T(8,128)(2,1)} %get-tuple-element.143, f32[2,512,2560]{2,1,0:T(8,128)S(1)} %get-tuple-element.113, f32[2,512]{1,0:T(2,128)S(1)} %get-tuple-element.114, pred[512,2560]{1,0:T(8,128)(4,1)S(1)} %broadcast_compare_fusion.2, f32[512,2]{0,1:T(2,128)S(1)} %bitcast.182), kind=kOutput, calls=%fused_computation.15.clone.1 | convolution fusion | flops 388120576 | bytes 12689408 | tf_op jit(solution)/shard_map/while/body/eval_jaxpr/hqk,khd->qhd/dot_general | solution.py:62
  179.7 0.8 broadcast_compare_fusion.2
  180.5 3.7 %fusion.103 = (f32[2,512]{1,0:T(2,128)S(1)}, f32[2,512,2560]{2,1,0:T(8,128)S(1)}) fusion(pred[512,2560]{1,0:T(8,128)(4,1)S(1)} %broadcast_compare_fusion.2, bf16[2560,2,72]{0,2,1:T(8,128)(2,1)} %get-tuple-element.142, bf16[2560,2,72]{0,2,1:T(8,128)(2,1)} %get-tuple-element.141, s32[]{:T(128)S(6)} %select_n.87), kind=kOutput, calls=%fused_computation.7.clone.1 | convolution fusion | flops 385350656 | bytes 12685316 | tf_op jit(solution)/shard_map/while/body/eval_jaxpr/qhd,khd->hqk/dot_general | solution.py:53
  184.2 3.0 %fusion.104 = f32[2,512]{1,0:T(2,128)S(1)} fusion(f32[2,512,2560]{2,1,0:T(8,128)S(1)} %get-tuple-element.113, f32[2,512]{1,0:T(2,128)S(1)} %get-tuple-element.114, pred[512,2560]{1,0:T(8,128)(4,1)S(1)} %broadcast_compare_fusion.2), kind=kLoop, calls=%fused_computation.8.clone.1 | loop fusion | flops 10484736 | bytes 11804672 | tf_op jit(solution)/shard_map/while/body/eval_jaxpr/reduce_sum | solution.py:60
  187.3 4.1 %fusion.105 = bf16[512,2,72]{0,2,1:T(8,128)(2,1)S(1)} fusion(bf16[2560,2,72]{0,2,1:T(8,128)(2,1)} %get-tuple-element.143, f32[2,512,2560]{2,1,0:T(8,128)S(1)} %get-tuple-element.113, f32[2,512]{1,0:T(2,128)S(1)} %get-tuple-element.114, pred[512,2560]{1,0:T(8,128)(4,1)S(1)} %broadcast_compare_fusion.2, f32[512,2]{0,1:T(2,128)S(1)} %bitcast.182), kind=kOutput, calls=%fused_computation.15.clone.1 | convolution fusion | flops 388120576 | bytes 12689408 | tf_op jit(solution)/shard_map/while/body/eval_jaxpr/hqk,khd->qhd/dot_general | solution.py:62
  193.3 0.8 broadcast_compare_fusion.2
  194.1 3.7 %fusion.103 = (f32[2,512]{1,0:T(2,128)S(1)}, f32[2,512,2560]{2,1,0:T(8,128)S(1)}) fusion(pred[512,2560]{1,0:T(8,128)(4,1)S(1)} %broadcast_compare_fusion.2, bf16[2560,2,72]{0,2,1:T(8,128)(2,1)} %get-tuple-element.142, bf16[2560,2,72]{0,2,1:T(8,128)(2,1)} %get-tuple-element.141, s32[]{:T(128)S(6)} %select_n.87), kind=kOutput, calls=%fused_computation.7.clone.1 | convolution fusion | flops 385350656 | bytes 12685316 | tf_op jit(solution)/shard_map/while/body/eval_jaxpr/qhd,khd->hqk/dot_general | solution.py:53
  197.8 3.0 %fusion.104 = f32[2,512]{1,0:T(2,128)S(1)} fusion(f32[2,512,2560]{2,1,0:T(8,128)S(1)} %get-tuple-element.113, f32[2,512]{1,0:T(2,128)S(1)} %get-tuple-element.114, pred[512,2560]{1,0:T(8,128)(4,1)S(1)} %broadcast_compare_fusion.2), kind=kLoop, calls=%fused_computation.8.clone.1 | loop fusion | flops 10484736 | bytes 11804672 | tf_op jit(solution)/shard_map/while/body/eval_jaxpr/reduce_sum | solution.py:60
  200.9 4.1 %fusion.105 = bf16[512,2,72]{0,2,1:T(8,128)(2,1)S(1)} fusion(bf16[2560,2,72]{0,2,1:T(8,128)(2,1)} %get-tuple-element.143, f32[2,512,2560]{2,1,0:T(8,128)S(1)} %get-tuple-element.113, f32[2,512]{1,0:T(2,128)S(1)} %get-tuple-element.114, pred[512,2560]{1,0:T(8,128)(4,1)S(1)} %broadcast_compare_fusion.2, f32[512,2]{0,1:T(2,128)S(1)} %bitcast.182), kind=kOutput, calls=%fused_computation.15.clone.1 | convolution fusion | flops 388120576 | bytes 12689408 | tf_op jit(solution)/shard_map/while/body/eval_jaxpr/hqk,khd->qhd/dot_general | solution.py:62
  205.6 2.6 copy.29
  208.3 2.8 %reshape_reshape.6 = bf16[2560,1,144]{0,2,1:T(8,128)(2,1)} reshape(bf16[5,512,144]{1,0,2:T(8,128)(2,1)} %copy.29) | data formatting | bytes 1474560 | tf_op jit(solution)/shard_map/reshape;reshape | solution.py:130
  211.1 0.9 fusion.66
  212.0 1.0 fusion.65
  213.0 0.9 fusion.64
  213.9 1.0 fusion.63
  215.0 0.9 fusion.62
  215.9 1.0 fusion.61
  216.9 0.9 fusion.60
  217.8 1.0 fusion.59
  218.8 26.3 %all_to_all.60 = bf16[8,320,1,144]{1,3,2,0:T(8,128)(2,1)S(1)} all-to-all(bf16[8,320,1,144]{1,3,2,0:T(8,128)(2,1)S(1)} %fusion.59), channel_id=1, replica_groups=mesh['bag'=4,'sp'=8] {'sp'}, dimensions={0} | all-to-all | bytes 1474560 | tf_op jit(solution)/shard_map/all_to_all | solution.py:89
  245.2 2.8 %fusion.85 = (f32[320]{0:T(512)S(1)}, f32[320,1152]{1,0:T(8,128)S(1)}) fusion(bf16[320,1152]{0,1:T(8,128)(2,1)S(1)} %bitcast.176, bf16[1152,1152]{1,0:T(8,128)(2,1)S(1)} %copy-done, f32[320,6,1152]{2,0,1:T(8,128)} %fusion.67, bf16[320,1152]{1,0:T(8,128)(2,1)S(1)} %bitcast.173), kind=kOutput, calls=%fused_computation.117 | convolution fusion | flops 851558080 | bytes 7079168 | tf_op jit(solution)/shard_map/dot_general | solution.py:71
  248.0 1.2 copy-done.4
  249.5 11.4 %fusion.30 = bf16[320,1152]{1,0:T(8,128)(2,1)} fusion(f32[320,1152]{1,0:T(8,128)} %copy-done.4, bf16[2304,1152]{1,0:T(8,128)(2,1)} %param.15, f32[320,6,1152]{2,0,1:T(8,128)} %fusion.67, bf16[1152,2304]{1,0:T(8,128)(2,1)} %param.14, f32[320]{0:T(512)S(1)} %add_rsqrt_fusion, f32[320]{0:T(512)S(1)} %broadcast_multiply_fusion), kind=kOutput, calls=%fused_computation.36 | convolution fusion | flops 3407339520 | bytes 18729472 | tf_op jit(solution)/shard_map/dot_general | solution.py:81
  260.9 3.5 %all-to-all-start.5 = ((bf16[4,80,1152]{2,1,0:T(8,128)(2,1)}), bf16[4,80,1152]{2,1,0:T(8,128)(2,1)S(1)}, u32[]{:S(2)}, u32[]{:S(2)}) async-start(bf16[4,80,1152]{2,1,0:T(8,128)(2,1)} %bitcast.181), calls=%async_computation.5 | async-start | bytes 1474560 | tf_op jit(solution)/shard_map/all_to_all | solution.py:132
  264.4 11.0 %all-to-all-done.5 = bf16[4,80,1152]{2,1,0:T(8,128)(2,1)S(1)} async-done(((bf16[4,80,1152]{2,1,0:T(8,128)(2,1)}), bf16[4,80,1152]{2,1,0:T(8,128)(2,1)S(1)}, u32[]{:S(2)}, u32[]{:S(2)}) %all-to-all-start.5) | async-done | bytes 737312 | tf_op jit(solution)/shard_map/all_to_all | solution.py:132
  275.4 2.1 gather_fusion.2
  277.5 2.0 broadcast_select_fusion
  (62 shorter events, 10.0 us)
Async XLA Ops:
  0.0 245.2 %copy-start = (bf16[1152,1152]{1,0:T(8,128)(2,1)S(1)}, bf16[1152,1152]{1,0:T(8,128)(2,1)}, u32[]{:S(2)}) copy-start(bf16[1152,1152]{1,0:T(8,128)(2,1)} %param.13) | copy-start | bytes 7962628
  0.0 15.5 %copy-start.1 = (bf16[256,1152]{1,0:T(8,128)(2,1)S(1)}, bf16[256,1152]{1,0:T(8,128)(2,1)}, u32[]{:S(2)}) copy-start(bf16[256,1152]{1,0:T(8,128)(2,1)} %param.9) | copy-start | bytes 1769476
  11.1 9.4 %all-to-all-start.1 = ((bf16[4,80,1]{1,2,0:T(2,128)(2,1)}), bf16[4,80,1]{1,2,0:T(2,128)(2,1)S(1)}, u32[]{:S(2)}, u32[]{:S(2)}) async-start(bf16[4,80,1]{1,2,0:T(2,128)(2,1)} %all_to_all.53), calls=%async_computation.1 | async-start | bytes 4096 | tf_op jit(solution)/shard_map/all_to_all | solution.py:116
  18.2 7.8 %copy-start.5 = (f32[4,6,1152]{2,0,1:T(4,128)S(1)}, f32[4,6,1152]{2,0,1:T(4,128)}, u32[]{:S(2)}) copy-start(f32[4,6,1152]{2,0,1:T(4,128)} %param.11) | copy-start | bytes 331780
  20.5 14.6 %all-to-all-start = ((bf16[4,80,1152]{2,1,0:T(8,128)(2,1)}), bf16[4,80,1152]{2,1,0:T(8,128)(2,1)S(1)}, u32[]{:S(2)}, u32[]{:S(2)}) async-start(bf16[4,80,1152]{2,1,0:T(8,128)(2,1)} %select_select_fusion), calls=%async_computation | async-start | bytes 1474560 | tf_op jit(solution)/shard_map/all_to_all | solution.py:115
  35.0 9.3 %copy-start.2 = (bf16[4,80,1152]{2,1,0:T(8,128)(2,1)}, bf16[4,80,1152]{2,1,0:T(8,128)(2,1)S(1)}, u32[]{:S(2)}) copy-start(bf16[4,80,1152]{2,1,0:T(8,128)(2,1)S(1)} %all-to-all-done) | copy-start | bytes 2211844
  35.0 25.0 %all-to-all-start.2 = ((bf16[8,2,160]{2,1,0:T(2,128)(2,1)}), bf16[8,2,160]{2,1,0:T(2,128)(2,1)S(1)}, u32[]{:S(2)}, u32[]{:S(2)}) async-start(bf16[8,2,160]{2,1,0:T(2,128)(2,1)} %reshape.216), calls=%async_computation.2 | async-start | bytes 16384 | tf_op jit(solution)/shard_map/all_to_all | solution.py:125
  60.0 65.4 %all-to-all-start.3 = ((bf16[320,3,8,144]{0,3,1,2:T(8,128)(2,1)}), bf16[320,3,8,144]{0,3,1,2:T(8,128)(2,1)}, u32[]{:S(2)}, u32[]{:S(2)}) async-start(bf16[320,3,8,144]{0,3,1,2:T(8,128)(2,1)} %copy.27), calls=%async_computation.3 | async-start | bytes 5308416 | tf_op jit(solution)/shard_map/all_to_all | solution.py:124
  208.3 36.9 %copy-start.3 = (bf16[4,80,1152]{2,1,0:T(8,128)(2,1)S(1)}, bf16[4,80,1152]{2,1,0:T(8,128)(2,1)}, u32[]{:S(2)}) copy-start(bf16[4,80,1152]{2,1,0:T(8,128)(2,1)} %copy-done.2) | copy-start | bytes 2211844
  248.0 1.2 copy-start.4
  260.9 14.6 %all-to-all-start.5 = ((bf16[4,80,1152]{2,1,0:T(8,128)(2,1)}), bf16[4,80,1152]{2,1,0:T(8,128)(2,1)S(1)}, u32[]{:S(2)}, u32[]{:S(2)}) async-start(bf16[4,80,1152]{2,1,0:T(8,128)(2,1)} %bitcast.181), calls=%async_computation.5 | async-start | bytes 1474560 | tf_op jit(solution)/shard_map/all_to_all | solution.py:132
